TPU v7x, 32 devices: a whole 2x2x4 slice. The times are simulated.
32 devices in a mesh: groups: 2 (over y), section: 4 (over z), replica: 4 (over x, core).
Axes of the slice: x: 2, y: 2, z: 4, core: 2. Of those that a mesh axis runs over, the one named last changes fastest.
Arguments:
- section_inputs: bfloat16 [8, 4, 2, 16, 16, 256], P(('groups', 'replica'), 'section'), parts along dimension 0, may hold values from -6 to 6
- cotangent: bfloat16 [8, 2, 16, 16, 256], P(('groups', 'replica')), parts along dimension 0, may hold values from -6 to 6
- crop_rows: int32 [8, 2], P(('groups', 'replica')), parts along dimension 0, may hold values from 0 to 705
- drift: bfloat16 [8, 4, 9, 256, 256], P(('groups', 'replica'), 'section'), parts along dimension 0, may hold values from -6 to 6
- params: float32 [8, 9, 256, 256], P(('groups', 'section')), parts along dimension 0, may hold values from -6 to 6
- momentum: float32 [8, 9, 256, 256], P(('groups', 'section'), None, 'replica'), parts along dimension 0, may hold values from -4 to 4
Outputs:
- new_params: float32 [8, 9, 256, 256], P(('groups', 'section')), parts along dimension 0
- new_momentum: float32 [8, 9, 256, 256], P(('groups', 'section'), None, 'replica'), parts along dimension 0
There are 2 independent parts, one for each index of `groups`. A program takes and returns all parts, laid end to end along the dimension named above; each array names one. Nothing has to cross between parts.
All inputs are finite; a program needn't handle non-finite values.
Results may differ from a plain program's by a relative error of at most 0.0075.
Values may be sent and summed in bfloat16 or wider, within the bound.
No kernel may reach another device: no remote copies, remote signals or barrier semaphores. Data moves between devices by JAX's collectives and lax.ppermute only.
A program may use at most 64 MiB of HBM per device.

v0:
```python
import math
import jax
import jax.numpy as jnp
from jax import lax
from jax.sharding import PartitionSpec as P

LATS = 721


def from_behind(x, axis, by):
    devices = lax.axis_size(axis)
    pairs = [(i, i + by) for i in range(devices) if 0 <= i + by < devices]
    return lax.ppermute(x, axis, pairs)


def lat_weight(first_row, count):
    rows = jnp.arange(count, dtype=jnp.float32) + first_row.astype(jnp.float32)
    middle = (LATS - 1) / 2.0
    every = jnp.arange(LATS, dtype=jnp.float32)
    norm_value = jnp.mean(jnp.cos(math.pi * (every - middle) / (LATS - 1)))
    return jnp.cos(math.pi * (rows - middle) / (LATS - 1)) / norm_value


def backward(inputs, out_grad, weights):
    rows, cols, width = inputs.shape
    scale = (9.0 * width) ** (-0.5)
    padded = jnp.pad(inputs, ((1, 1), (1, 1), (0, 0)))
    taps = jnp.stack([padded[a : a + rows, b : b + cols] for a in range(3) for b in range(3)])
    pre = jnp.einsum("krcd,kde->rce", taps, weights, preferred_element_type=jnp.float32) * scale
    tangent = jnp.tanh(pre)
    local = (out_grad.astype(jnp.float32) * (1.0 - tangent * tangent)).astype(jnp.bfloat16)
    grad = jnp.einsum("krcd,rce->kde", taps, local, preferred_element_type=jnp.float32) * scale
    back = jnp.einsum("rce,kde->krcd", local, weights, preferred_element_type=jnp.float32)
    accum = jnp.zeros((rows + 2, cols + 2, width), jnp.float32)
    for a in range(3):
        for b in range(3):
            accum = accum.at[a : a + rows, b : b + cols].add(back[3 * a + b])
    in_grad = (out_grad.astype(jnp.float32) + scale * accum[1 : rows + 1, 1 : cols + 1]).astype(
        jnp.bfloat16
    )
    return (grad, in_grad)


def per_device(section_inputs, cotangent, crop_rows, drift, params, momentum):
    section = lax.axis_index("section")
    sections = lax.axis_size("section")
    inputs_here = section_inputs[0, 0]
    cot_here = cotangent[0]
    crops_here = crop_rows[0]
    micro = inputs_here.shape[0]
    rows, cols, width = inputs_here.shape[1:]
    weights_bf = params[0].astype(jnp.bfloat16)

    def tick(step, carry):
        incoming, grad_total = carry
        micro_index = step - (sections - 1 - section)
        valid = jnp.logical_and(micro_index >= 0, micro_index < micro)
        chosen = jnp.clip(micro_index, 0, micro - 1)
        inputs_now = lax.dynamic_index_in_dim(inputs_here, chosen, 0, keepdims=False)
        cot_now = lax.dynamic_index_in_dim(cot_here, chosen, 0, keepdims=False)
        first_row = lax.dynamic_index_in_dim(crops_here, chosen, 0, keepdims=False)
        top_grad = (
            cot_now.astype(jnp.float32) * lat_weight(first_row, rows)[:, None, None]
        ).astype(jnp.bfloat16)
        out_grad = jnp.where(section == sections - 1, top_grad, incoming)
        contrib, in_grad = backward(inputs_now, out_grad, weights_bf)
        grad_total = grad_total + jnp.where(valid, contrib, jnp.zeros_like(contrib))
        passed = from_behind(in_grad, "section", -1)
        return (passed, grad_total)

    start = (
        jnp.zeros((rows, cols, width), jnp.bfloat16),
        jnp.zeros((9, width, width), jnp.float32),
    )
    unused, grad_total = lax.fori_loop(0, sections + micro - 1, tick, start)
    delta_bf = (drift[0, 0].astype(jnp.float32) + 0.5 * grad_total).astype(jnp.bfloat16)
    delta_bf = lax.optimization_barrier(delta_bf)
    delta = delta_bf.astype(jnp.float32)
    replicas = lax.axis_size("replica")
    here = lax.axis_index("replica")
    share_rows = width // replicas
    mean_delta = lax.psum(delta.astype(jnp.bfloat16), "replica").astype(jnp.float32) / replicas
    mom_whole = lax.all_gather(momentum[0], "replica", axis=1, tiled=True)
    mom_next = 0.9 * mom_whole + mean_delta
    new_params = params[0] - 0.7 * (mean_delta + 0.9 * mom_next)
    new_momentum = lax.dynamic_slice_in_dim(mom_next, here * share_rows, share_rows, 1)
    return (new_params[None], new_momentum[None])


def solution(mesh):
    placed = (
        P(("groups", "replica"), "section", None, None, None, None),
        P(("groups", "replica"), None, None, None, None),
        P(("groups", "replica"), None),
        P(("groups", "replica"), "section", None, None, None),
        P(("groups", "section"), None, None, None),
        P(("groups", "section"), None, "replica", None),
    )
    return jax.shard_map(
        per_device,
        mesh=mesh,
        in_specs=placed,
        out_specs=(
            P(("groups", "section"), None, None, None),
            P(("groups", "section"), None, "replica", None),
        ),
        check_vma=False,
    )
```

profile of v0, /device:TPU:0, one launch (start us, length us, event | category | flops | bytes accessed | tf_op | source)
XLA Modules:
  0.0 208.0 jit_solution(15496415123760340458)
XLA Ops:
  7.3 1.8 bitcast_convert_fusion
  9.1 119.2 %while.28 = (s32[]{:T(128)}, bf16[16,16,256]{2,1,0:T(8,128)(2,1)S(1)}, f32[9,256,256]{2,1,0:T(8,128)}, pred[]{:T(512)}, s32[]{:T(128)}, /*index=5*/bf16[2,16,16,...) while((s32[]{:T(128)}, ...), condition=%wide.region_3.4_spmd.clone, body=%wide.region_0.3_spmd.clone.sunk | while | flops 910100672 | bytes 44110644 | solution.py:75
  17.2 1.6 scatter-add.71
  19.5 1.9 add_select_fusion.2
  21.4 1.6 scatter-add.72
  27.2 3.4 %fusion.113 = f32[9,256,256]{2,1,0:T(8,128)} fusion(f32[9,256,256]{2,1,0:T(8,128)} %get-tuple-element.608, bf16[9,16,16,256]{3,2,0,1:T(8,128)(2,1)} %copy-done.7, pred[]{:T(512)S(6)} %compare.180, pred[]{:T(512)S(6)} %and.113, bf16[16,16,256]{2,1,0:T(8,128)(2,1)} %copy-done.6), kind=kOutput, calls=%fused_computation.2.clone.1 | convolution fusion | flops 304349184 | bytes 6029314 | tf_op jit(solution)/shard_map/while/body/eval_jaxpr/krcd,rce->kde/dot_general | solution.py:32
  30.6 3.7 %collective-permute-done = bf16[16,16,256]{2,1,0:T(8,128)(2,1)S(1)} collective-permute-done((bf16[16,16,256]{2,1,0:T(8,128)(2,1)S(1)}, bf16[16,16,256]{2,1,0:T(8,128)(2,1)S(1)}, u32[]{:S(2)}, u32[]{:S(2)}) %collective-permute-start) | collective-permute-done | bytes 131104 | tf_op jit(solution)/shard_map/while/body/eval_jaxpr/ppermute | solution.py:13
  42.3 1.6 scatter-add.71
  44.6 1.9 add_select_fusion.2
  46.5 1.6 scatter-add.72
  52.3 4.2 %fusion.113 = f32[9,256,256]{2,1,0:T(8,128)} fusion(f32[9,256,256]{2,1,0:T(8,128)} %get-tuple-element.608, bf16[9,16,16,256]{3,2,0,1:T(8,128)(2,1)} %copy-done.7, pred[]{:T(512)S(6)} %compare.180, pred[]{:T(512)S(6)} %and.113, bf16[16,16,256]{2,1,0:T(8,128)(2,1)} %copy-done.6), kind=kOutput, calls=%fused_computation.2.clone.1 | convolution fusion | flops 304349184 | bytes 6029314 | tf_op jit(solution)/shard_map/while/body/eval_jaxpr/krcd,rce->kde/dot_general | solution.py:32
  65.8 1.6 scatter-add.71
  68.2 1.9 add_select_fusion.2
  75.8 4.2 %fusion.113 = f32[9,256,256]{2,1,0:T(8,128)} fusion(f32[9,256,256]{2,1,0:T(8,128)} %get-tuple-element.608, bf16[9,16,16,256]{3,2,0,1:T(8,128)(2,1)} %copy-done.7, pred[]{:T(512)S(6)} %compare.180, pred[]{:T(512)S(6)} %and.113, bf16[16,16,256]{2,1,0:T(8,128)(2,1)} %copy-done.6), kind=kOutput, calls=%fused_computation.2.clone.1 | convolution fusion | flops 304349184 | bytes 6029314 | tf_op jit(solution)/shard_map/while/body/eval_jaxpr/krcd,rce->kde/dot_general | solution.py:32
  89.3 1.6 scatter-add.71
  91.7 1.9 add_select_fusion.2
  99.3 4.2 %fusion.113 = f32[9,256,256]{2,1,0:T(8,128)} fusion(f32[9,256,256]{2,1,0:T(8,128)} %get-tuple-element.608, bf16[9,16,16,256]{3,2,0,1:T(8,128)(2,1)} %copy-done.7, pred[]{:T(512)S(6)} %compare.180, pred[]{:T(512)S(6)} %and.113, bf16[16,16,256]{2,1,0:T(8,128)(2,1)} %copy-done.6), kind=kOutput, calls=%fused_computation.2.clone.1 | convolution fusion | flops 304349184 | bytes 6029314 | tf_op jit(solution)/shard_map/while/body/eval_jaxpr/krcd,rce->kde/dot_general | solution.py:32
  112.9 1.6 scatter-add.71
  115.2 1.9 add_select_fusion.2
  122.9 4.2 %fusion.113 = f32[9,256,256]{2,1,0:T(8,128)} fusion(f32[9,256,256]{2,1,0:T(8,128)} %get-tuple-element.608, bf16[9,16,16,256]{3,2,0,1:T(8,128)(2,1)} %copy-done.7, pred[]{:T(512)S(6)} %compare.180, pred[]{:T(512)S(6)} %and.113, bf16[16,16,256]{2,1,0:T(8,128)(2,1)} %copy-done.6), kind=kOutput, calls=%fused_computation.2.clone.1 | convolution fusion | flops 304349184 | bytes 6029314 | tf_op jit(solution)/shard_map/while/body/eval_jaxpr/krcd,rce->kde/dot_general | solution.py:32
  128.4 3.5 %fusion.56 = bf16[9,256,256]{2,1,0:T(8,128)(2,1)} fusion(f32[9,256,256]{2,1,0:T(8,128)} %get-tuple-element.472, bf16[1,1,9,256,256]{4,3,2,1,0:T(8,128)(2,1)} %param.29), kind=kLoop, calls=%fused_computation.72 | loop fusion | flops 2359296 | bytes 4718592 | tf_op jit(solution)/shard_map/convert_element_type | solution.py:76
  132.6 37.8 %all-reduce.4.cloned.1.call-done = bf16[9,256,256]{2,1,0:T(8,128)(2,1)} async-done(((bf16[9,256,256]{2,1,0:T(8,128)(2,1)}), bf16[9,256,256]{2,1,0:T(8,128)(2,1)}) %all-reduce.4.cloned.1.call-update) | async-done | bytes 1179664 | tf_op jit(solution)/shard_map/psum | solution.py:82
  170.5 25.8 %all-gather.3.cloned.1.call-done = f32[1,9,256,256]{3,2,1,0:T(8,128)} async-done(((f32[1,9,64,256]{3,2,1,0:T(8,128)}), f32[1,9,256,256]{3,2,1,0:T(8,128)}) %all-gather.3.cloned.1.call-update) | async-done | bytes 2359312 | tf_op jit(solution)/shard_map/all_gather | solution.py:83
  196.3 4.0 %bitcast_add_fusion = (f32[9,256,256]{2,1,0:T(8,128)S(1)}, f32[1,9,256,256]{3,2,1,0:T(8,128)}) fusion(f32[1,9,256,256]{3,2,1,0:T(8,128)} %all-gather.3.cloned.1.call-done, bf16[9,256,256]{2,1,0:T(8,128)(2,1)} %all-reduce.4.cloned.1.call-done, f32[1,9,256,256]{3,2,1,0:T(8,128)S(1)} %copy-done.4), kind=kLoop, calls=%fused_computation.73 | loop fusion | flops 4718592 | bytes 10616832 | tf_op jit(solution)/shard_map/add | solution.py:84
  (268 shorter events, 68.3 us)
Async XLA Ops:
  7.2 163.3 %all-reduce.4.cloned.1.call-start = ((), (), s32[]{:S(2)}) async-start(), calls=%async_computation | async-start | bytes 2359296 | tf_op jit(solution)/shard_map/psum | solution.py:82
  9.2 3.4 %copy-start.2 = (bf16[2,16,16,256]{3,2,0,1:T(8,128)(2,1)}, bf16[2,16,16,256]{3,2,0,1:T(8,128)(2,1)S(1)}, u32[]{:S(2)}) copy-start(bf16[2,16,16,256]{3,2,0,1:T(8,128)(2,1)S(1)} %get-tuple-element.629) | copy-start | bytes 786436 | tf_op jit(solution)/shard_map/while
  9.2 4.8 %copy-start = (bf16[9,256,256]{2,1,0:T(8,128)(2,1)}, bf16[9,256,256]{2,1,0:T(8,128)(2,1)S(1)}, u32[]{:S(2)}) copy-start(bf16[9,256,256]{2,1,0:T(8,128)(2,1)S(1)} %get-tuple-element.630) | copy-start | bytes 3538948 | tf_op jit(solution)/shard_map/while
  25.8 8.4 %collective-permute-start = (bf16[16,16,256]{2,1,0:T(8,128)(2,1)S(1)}, bf16[16,16,256]{2,1,0:T(8,128)(2,1)S(1)}, u32[]{:S(2)}, u32[]{:S(2)}) collective-permute-start(bf16[16,16,256]{2,1,0:T(8,128)(2,1)S(1)} %fusion.112), channel_id=1, source_target_pairs={{4,0},{8,4},{12,8},{5,1},{9,5},{13,9},{6,2},{10,6},{14,10},{7,3},{... | collective-permute-start | bytes 393224 | tf_op jit(solution)/shard_map/while/body/eval_jaxpr/ppermute | solution.py:13
  27.2 7.1 %copy-start.1 = (bf16[9,256,256]{2,1,0:T(8,128)(2,1)S(1)}, bf16[9,256,256]{2,1,0:T(8,128)(2,1)}, u32[]{:S(2)}) copy-start(bf16[9,256,256]{2,1,0:T(8,128)(2,1)} %copy-done) | copy-start | bytes 3538948 | tf_op jit(solution)/shard_map/while
  27.2 7.1 %copy-start.3 = (bf16[2,16,16,256]{3,2,0,1:T(8,128)(2,1)S(1)}, bf16[2,16,16,256]{3,2,0,1:T(8,128)(2,1)}, u32[]{:S(2)}) copy-start(bf16[2,16,16,256]{3,2,0,1:T(8,128)(2,1)} %copy-done.2) | copy-start | bytes 786436 | tf_op jit(solution)/shard_map/while
  34.3 4.8 %copy-start = (bf16[9,256,256]{2,1,0:T(8,128)(2,1)}, bf16[9,256,256]{2,1,0:T(8,128)(2,1)S(1)}, u32[]{:S(2)}) copy-start(bf16[9,256,256]{2,1,0:T(8,128)(2,1)S(1)} %get-tuple-element.630) | copy-start | bytes 3538948 | tf_op jit(solution)/shard_map/while
  50.9 6.9 %collective-permute-start = (bf16[16,16,256]{2,1,0:T(8,128)(2,1)S(1)}, bf16[16,16,256]{2,1,0:T(8,128)(2,1)S(1)}, u32[]{:S(2)}, u32[]{:S(2)}) collective-permute-start(bf16[16,16,256]{2,1,0:T(8,128)(2,1)S(1)} %fusion.112), channel_id=1, source_target_pairs={{4,0},{8,4},{12,8},{5,1},{9,5},{13,9},{6,2},{10,6},{14,10},{7,3},{... | collective-permute-start | bytes 393224 | tf_op jit(solution)/shard_map/while/body/eval_jaxpr/ppermute | solution.py:13
  52.2 5.6 %copy-start.1 = (bf16[9,256,256]{2,1,0:T(8,128)(2,1)S(1)}, bf16[9,256,256]{2,1,0:T(8,128)(2,1)}, u32[]{:S(2)}) copy-start(bf16[9,256,256]{2,1,0:T(8,128)(2,1)} %copy-done) | copy-start | bytes 3538948 | tf_op jit(solution)/shard_map/while
  52.3 5.5 %copy-start.3 = (bf16[2,16,16,256]{3,2,0,1:T(8,128)(2,1)S(1)}, bf16[2,16,16,256]{3,2,0,1:T(8,128)(2,1)}, u32[]{:S(2)}) copy-start(bf16[2,16,16,256]{3,2,0,1:T(8,128)(2,1)} %copy-done.2) | copy-start | bytes 786436 | tf_op jit(solution)/shard_map/while
  57.8 4.8 %copy-start = (bf16[9,256,256]{2,1,0:T(8,128)(2,1)}, bf16[9,256,256]{2,1,0:T(8,128)(2,1)S(1)}, u32[]{:S(2)}) copy-start(bf16[9,256,256]{2,1,0:T(8,128)(2,1)S(1)} %get-tuple-element.630) | copy-start | bytes 3538948 | tf_op jit(solution)/shard_map/while
  74.5 6.9 %collective-permute-start = (bf16[16,16,256]{2,1,0:T(8,128)(2,1)S(1)}, bf16[16,16,256]{2,1,0:T(8,128)(2,1)S(1)}, u32[]{:S(2)}, u32[]{:S(2)}) collective-permute-start(bf16[16,16,256]{2,1,0:T(8,128)(2,1)S(1)} %fusion.112), channel_id=1, source_target_pairs={{4,0},{8,4},{12,8},{5,1},{9,5},{13,9},{6,2},{10,6},{14,10},{7,3},{... | collective-permute-start | bytes 393224 | tf_op jit(solution)/shard_map/while/body/eval_jaxpr/ppermute | solution.py:13
  75.8 5.6 %copy-start.1 = (bf16[9,256,256]{2,1,0:T(8,128)(2,1)S(1)}, bf16[9,256,256]{2,1,0:T(8,128)(2,1)}, u32[]{:S(2)}) copy-start(bf16[9,256,256]{2,1,0:T(8,128)(2,1)} %copy-done) | copy-start | bytes 3538948 | tf_op jit(solution)/shard_map/while
  75.8 5.5 %copy-start.3 = (bf16[2,16,16,256]{3,2,0,1:T(8,128)(2,1)S(1)}, bf16[2,16,16,256]{3,2,0,1:T(8,128)(2,1)}, u32[]{:S(2)}) copy-start(bf16[2,16,16,256]{3,2,0,1:T(8,128)(2,1)} %copy-done.2) | copy-start | bytes 786436 | tf_op jit(solution)/shard_map/while
  81.3 4.8 %copy-start = (bf16[9,256,256]{2,1,0:T(8,128)(2,1)}, bf16[9,256,256]{2,1,0:T(8,128)(2,1)S(1)}, u32[]{:S(2)}) copy-start(bf16[9,256,256]{2,1,0:T(8,128)(2,1)S(1)} %get-tuple-element.630) | copy-start | bytes 3538948 | tf_op jit(solution)/shard_map/while
  98.0 6.9 %collective-permute-start = (bf16[16,16,256]{2,1,0:T(8,128)(2,1)S(1)}, bf16[16,16,256]{2,1,0:T(8,128)(2,1)S(1)}, u32[]{:S(2)}, u32[]{:S(2)}) collective-permute-start(bf16[16,16,256]{2,1,0:T(8,128)(2,1)S(1)} %fusion.112), channel_id=1, source_target_pairs={{4,0},{8,4},{12,8},{5,1},{9,5},{13,9},{6,2},{10,6},{14,10},{7,3},{... | collective-permute-start | bytes 393224 | tf_op jit(solution)/shard_map/while/body/eval_jaxpr/ppermute | solution.py:13
  99.3 5.6 %copy-start.1 = (bf16[9,256,256]{2,1,0:T(8,128)(2,1)S(1)}, bf16[9,256,256]{2,1,0:T(8,128)(2,1)}, u32[]{:S(2)}) copy-start(bf16[9,256,256]{2,1,0:T(8,128)(2,1)} %copy-done) | copy-start | bytes 3538948 | tf_op jit(solution)/shard_map/while
  99.3 5.5 %copy-start.3 = (bf16[2,16,16,256]{3,2,0,1:T(8,128)(2,1)S(1)}, bf16[2,16,16,256]{3,2,0,1:T(8,128)(2,1)}, u32[]{:S(2)}) copy-start(bf16[2,16,16,256]{3,2,0,1:T(8,128)(2,1)} %copy-done.2) | copy-start | bytes 786436 | tf_op jit(solution)/shard_map/while
  104.9 4.8 %copy-start = (bf16[9,256,256]{2,1,0:T(8,128)(2,1)}, bf16[9,256,256]{2,1,0:T(8,128)(2,1)S(1)}, u32[]{:S(2)}) copy-start(bf16[9,256,256]{2,1,0:T(8,128)(2,1)S(1)} %get-tuple-element.630) | copy-start | bytes 3538948 | tf_op jit(solution)/shard_map/while
  121.5 6.9 %collective-permute-start = (bf16[16,16,256]{2,1,0:T(8,128)(2,1)S(1)}, bf16[16,16,256]{2,1,0:T(8,128)(2,1)S(1)}, u32[]{:S(2)}, u32[]{:S(2)}) collective-permute-start(bf16[16,16,256]{2,1,0:T(8,128)(2,1)S(1)} %fusion.112), channel_id=1, source_target_pairs={{4,0},{8,4},{12,8},{5,1},{9,5},{13,9},{6,2},{10,6},{14,10},{7,3},{... | collective-permute-start | bytes 393224 | tf_op jit(solution)/shard_map/while/body/eval_jaxpr/ppermute | solution.py:13
  122.8 5.6 %copy-start.1 = (bf16[9,256,256]{2,1,0:T(8,128)(2,1)S(1)}, bf16[9,256,256]{2,1,0:T(8,128)(2,1)}, u32[]{:S(2)}) copy-start(bf16[9,256,256]{2,1,0:T(8,128)(2,1)} %copy-done) | copy-start | bytes 3538948 | tf_op jit(solution)/shard_map/while
  122.9 5.5 %copy-start.3 = (bf16[2,16,16,256]{3,2,0,1:T(8,128)(2,1)S(1)}, bf16[2,16,16,256]{3,2,0,1:T(8,128)(2,1)}, u32[]{:S(2)}) copy-start(bf16[2,16,16,256]{3,2,0,1:T(8,128)(2,1)} %copy-done.2) | copy-start | bytes 786436 | tf_op jit(solution)/shard_map/while
  128.4 67.9 %copy-start.4 = (f32[1,9,256,256]{3,2,1,0:T(8,128)S(1)}, f32[1,9,256,256]{3,2,1,0:T(8,128)}, u32[]{:S(2)}) copy-start(f32[1,9,256,256]{3,2,1,0:T(8,128)} %param.30) | copy-start | bytes 7077892
  131.9 64.4 %all-gather.3.cloned.1.call-start = ((), (), s32[]{:S(2)}) async-start(), calls=%async_computation.1 | async-start | bytes 2949120 | tf_op jit(solution)/shard_map/all_gather | solution.py:83
  (22 other events, 56.1 us)
Sparse Core Ops, SparseCore 0:
  132.0 38.4 all-reduce.3
  172.0 24.1 all-gather.2
where the time goes:
time: 209 us; the launch traced here: 208 us
  waiting for transfers between devices  73.4 us (35%)
  other arithmetic  40.8 us (20%)
  local copies, waits for them, and re-layouts  35.3 us (17%)
  matrix products  29.7 us (14%)
  between operations  14.1 us (7%)
  loops' own time  8.19 us (4%)
  starting transfers between devices  6.54 us (3%)
    psum x1, waiting for transfers between devices, per_device(): lax.psum(delta.astype(jnp.bfloat16), 'replica').astype(jnp.float32)  37.8 us
    all_gather x1, waiting for transfers between devices, per_device(): mom_whole = lax.all_gather(momentum[0], 'replica', axis=1, tiled=True)  25.8 us
    scatter-add x35, local copies, waits for them, and re-layouts, backward(): accum = accum.at[a:a + rows, b:b + cols].add(back[3 * a + b])  22.7 us
    dot_general x5, matrix products, backward(): jnp.einsum('krcd,rce->kde', taps, local, preferred_element_type=jnp.float32)  20.2 us
    another operation x15, other arithmetic  13.3 us
    ppermute x5, waiting for transfers between devices, from_behind(): return lax.ppermute(x, axis, pairs)  9.02 us
    another operation x1, loops' own time, per_device(): unused, grad_total = lax.fori_loop(0, sections + micro - 1, tick, start)  8.19 us
    add x25, other arithmetic, backward(): accum = accum.at[a:a + rows, b:b + cols].add(back[3 * a + b])  7.39 us
  transfers between devices with their start and end apart: 7, of which 7 were waited for; matrix products, arithmetic and copies ran while one was open for 10% of the time, Pallas kernels for 0%

commit v1 on v0

--- a/solution.py
+++ b/solution.py
@@ -5,6 +5,23 @@
 from jax.sharding import PartitionSpec as P
 
 LATS = 721
+
+
+def in_order(blocks, dim):
+    shape = list(blocks.shape[1:])
+    shape[dim] *= blocks.shape[0]
+    return jnp.moveaxis(blocks, 0, dim).reshape(shape)
+
+
+def collected_by_bits(value, axis):
+    devices, position = (lax.axis_size(axis), lax.axis_index(axis))
+    pieces, apart = (value[None], 1)
+    while apart < devices:
+        other = lax.ppermute(pieces, axis, [(i, i ^ apart) for i in range(devices)])
+        low = position & apart == 0
+        pieces = jnp.concatenate([jnp.where(low, pieces, other), jnp.where(low, other, pieces)])
+        apart *= 2
+    return pieces
 
 
 def from_behind(x, axis, by):
@@ -80,7 +97,7 @@
     here = lax.axis_index("replica")
     share_rows = width // replicas
     mean_delta = lax.psum(delta.astype(jnp.bfloat16), "replica").astype(jnp.float32) / replicas
-    mom_whole = lax.all_gather(momentum[0], "replica", axis=1, tiled=True)
+    mom_whole = in_order(collected_by_bits(momentum[0], "replica"), 1)
     mom_next = 0.9 * mom_whole + mean_delta
     new_params = params[0] - 0.7 * (mean_delta + 0.9 * mom_next)
     new_momentum = lax.dynamic_slice_in_dim(mom_next, here * share_rows, share_rows, 1)

time: 209 us -> 188 us (0.90)
  waiting for transfers between devices: 73.4 us -> 42.2 us
  local copies, waits for them, and re-layouts: 35.3 us -> 40.1 us
  other arithmetic: 40.8 us -> 44.5 us
  starting transfers between devices: 6.54 us -> 9.54 us
    all_gather x1 -> x0, waiting for transfers between devices: 25.8 us -> none  [per_device(): mom_whole = lax.all_gather(momentum[0], 'replica', axis=1, tiled=True)]
    psum x1, waiting for transfers between devices: 37.8 us -> 32.4 us  [per_device(): lax.psum(delta.astype(jnp.bfloat16), 'replica').astype(jnp.float32)]
    ppermute x0 -> x2, starting transfers between devices: none -> 3.05 us  [collected_by_bits(): other = lax.ppermute(pieces, axis, [(i, i ^ apart) for i in range(devices)])]
    select_n x0 -> x2, other arithmetic: none -> 2.66 us  [collected_by_bits(): jnp.where(low, pieces, other)]
    unnamed x9 -> x17, local copies, waits for them, and re-layouts: 0.04 us -> 2.27 us
  transfers between devices with their start and end apart: 7 -> 8, of which waited for: 7 -> 6; matrix products, arithmetic and copies ran while one was open for 10% -> 55% of each run, Pallas kernels for 0% -> 0%
where the time goes in v1:
time: 188 us; the launch traced here: 187 us
  other arithmetic  44.5 us (24%)
  waiting for transfers between devices  42.2 us (22%)
  local copies, waits for them, and re-layouts  40.1 us (21%)
  matrix products  28 us (15%)
  between operations  14.2 us (8%)
  starting transfers between devices  9.54 us (5%)
  loops' own time  8.32 us (4%)
    psum x1, waiting for transfers between devices, per_device(): lax.psum(delta.astype(jnp.bfloat16), 'replica').astype(jnp.float32)  32.4 us
    scatter-add x35, local copies, waits for them, and re-layouts, backward(): accum = accum.at[a:a + rows, b:b + cols].add(back[3 * a + b])  23.1 us
    dot_general x5, matrix products, backward(): jnp.einsum('krcd,rce->kde', taps, local, preferred_element_type=jnp.float32)  18.5 us
    another operation x15, other arithmetic  13.6 us
    ppermute x5, waiting for transfers between devices, from_behind(): return lax.ppermute(x, axis, pairs)  9.75 us
    another operation x1, loops' own time, per_device(): unused, grad_total = lax.fori_loop(0, sections + micro - 1, tick, start)  8.32 us
    add x25, other arithmetic, backward(): accum = accum.at[a:a + rows, b:b + cols].add(back[3 * a + b])  7.38 us
    dot_general x5, matrix products, backward(): jnp.einsum('krcd,kde->rce', taps, weights, preferred_element_type=jnp.flo...  7.01 us
  transfers between devices with their start and end apart: 8, of which 6 were waited for; matrix products, arithmetic and copies ran while one was open for 55% of the time, Pallas kernels for 0%

profile of v1, /device:TPU:0, one launch (start us, length us, event | category | flops | bytes accessed | tf_op | source)
XLA Modules:
  0.0 186.8 jit_solution(7561834137494741245)
XLA Ops:
  8.7 1.9 bitcast_convert_fusion
  13.2 2.5 %collective-permute-start.2 = (f32[2,9,64,256]{3,2,1,0:T(8,128)}, f32[2,9,64,256]{3,2,1,0:T(8,128)}, u32[]{:S(2)}, u32[]{:S(2)}) collective-permute-start(f32[2,9,64,256]{3,2,1,0:T(8,128)} %pad_maximum_fusion), channel_id=1, source_target_pairs={{0,2},{1,3},{2,0},{3,1},{4,6},{5,7},{6,4},{7,5},{8,10},{9,11},{10,... | collective-permute-start | bytes 3538952 | tf_op jit(solution)/shard_map/ppermute | solution.py:20
  15.7 119.0 %while.28 = (s32[]{:T(128)}, bf16[16,16,256]{2,1,0:T(8,128)(2,1)S(1)}, f32[9,256,256]{2,1,0:T(8,128)}, pred[]{:T(512)}, s32[]{:T(128)}, /*index=5*/bf16[2,16,16,...) while((s32[]{:T(128)}, ...), condition=%wide.region_3.4_spmd.clone, body=%wide.region_0.3_spmd.clone.sunk | while | flops 910100672 | bytes 49877872 | solution.py:92
  26.0 2.0 %add_select_fusion.2 = f32[16,16,256]{2,1,0:T(8,128)S(1)} fusion(f32[9,16,16,256]{3,2,1,0:T(8,128)S(1)} %convolution_bitcast_fusion.2, f32[18,18,256]{2,1,0:T(8,128)S(1)} %scatter-add.71, s32[]{:T(128)} %bitcast.241, s32[]{:T(128)} %bitcast.242, pred[]{:T(512)} %and_reduce_fusion.2), kind=kLoop, calls=%fused_computation.14.clone.1 | loop fusion | flops 131072 | bytes 786441 | tf_op jit(solution)/shard_map/select.79
  28.0 1.6 scatter-add.72
  33.9 3.0 %fusion.114 = f32[9,256,256]{2,1,0:T(8,128)} fusion(f32[9,256,256]{2,1,0:T(8,128)} %get-tuple-element.612, bf16[9,16,16,256]{3,2,0,1:T(8,128)(2,1)S(1)} %copy-done.14, pred[]{:T(512)S(6)} %compare.180, pred[]{:T(512)S(6)} %and.121, bf16[16,16,256]{2,1,0:T(8,128)(2,1)} %copy-done.10), kind=kOutput, calls=%fused_computation.2.clone.1 | convolution fusion | flops 304349184 | bytes 6029314 | tf_op jit(solution)/shard_map/while/body/eval_jaxpr/krcd,rce->kde/dot_general | solution.py:49
  36.9 3.1 %collective-permute-done = bf16[16,16,256]{2,1,0:T(8,128)(2,1)S(1)} collective-permute-done((bf16[16,16,256]{2,1,0:T(8,128)(2,1)S(1)}, bf16[16,16,256]{2,1,0:T(8,128)(2,1)S(1)}, u32[]{:S(2)}, u32[]{:S(2)}) %collective-permute-start) | collective-permute-done | bytes 131104 | tf_op jit(solution)/shard_map/while/body/eval_jaxpr/ppermute | solution.py:30
  50.3 2.0 %add_select_fusion.2 = f32[16,16,256]{2,1,0:T(8,128)S(1)} fusion(f32[9,16,16,256]{3,2,1,0:T(8,128)S(1)} %convolution_bitcast_fusion.2, f32[18,18,256]{2,1,0:T(8,128)S(1)} %scatter-add.71, s32[]{:T(128)} %bitcast.241, s32[]{:T(128)} %bitcast.242, pred[]{:T(512)} %and_reduce_fusion.2), kind=kLoop, calls=%fused_computation.14.clone.1 | loop fusion | flops 131072 | bytes 786441 | tf_op jit(solution)/shard_map/select.79
  52.3 1.6 scatter-add.72
  58.2 3.9 %fusion.114 = f32[9,256,256]{2,1,0:T(8,128)} fusion(f32[9,256,256]{2,1,0:T(8,128)} %get-tuple-element.612, bf16[9,16,16,256]{3,2,0,1:T(8,128)(2,1)S(1)} %copy-done.14, pred[]{:T(512)S(6)} %compare.180, pred[]{:T(512)S(6)} %and.121, bf16[16,16,256]{2,1,0:T(8,128)(2,1)} %copy-done.10), kind=kOutput, calls=%fused_computation.2.clone.1 | convolution fusion | flops 304349184 | bytes 6029314 | tf_op jit(solution)/shard_map/while/body/eval_jaxpr/krcd,rce->kde/dot_general | solution.py:49
  62.0 1.7 collective-permute-done
  73.9 2.0 %add_select_fusion.2 = f32[16,16,256]{2,1,0:T(8,128)S(1)} fusion(f32[9,16,16,256]{3,2,1,0:T(8,128)S(1)} %convolution_bitcast_fusion.2, f32[18,18,256]{2,1,0:T(8,128)S(1)} %scatter-add.71, s32[]{:T(128)} %bitcast.241, s32[]{:T(128)} %bitcast.242, pred[]{:T(512)} %and_reduce_fusion.2), kind=kLoop, calls=%fused_computation.14.clone.1 | loop fusion | flops 131072 | bytes 786441 | tf_op jit(solution)/shard_map/select.79
  81.8 3.9 %fusion.114 = f32[9,256,256]{2,1,0:T(8,128)} fusion(f32[9,256,256]{2,1,0:T(8,128)} %get-tuple-element.612, bf16[9,16,16,256]{3,2,0,1:T(8,128)(2,1)S(1)} %copy-done.14, pred[]{:T(512)S(6)} %compare.180, pred[]{:T(512)S(6)} %and.121, bf16[16,16,256]{2,1,0:T(8,128)(2,1)} %copy-done.10), kind=kOutput, calls=%fused_computation.2.clone.1 | convolution fusion | flops 304349184 | bytes 6029314 | tf_op jit(solution)/shard_map/while/body/eval_jaxpr/krcd,rce->kde/dot_general | solution.py:49
  85.7 1.7 collective-permute-done
  97.6 2.0 %add_select_fusion.2 = f32[16,16,256]{2,1,0:T(8,128)S(1)} fusion(f32[9,16,16,256]{3,2,1,0:T(8,128)S(1)} %convolution_bitcast_fusion.2, f32[18,18,256]{2,1,0:T(8,128)S(1)} %scatter-add.71, s32[]{:T(128)} %bitcast.241, s32[]{:T(128)} %bitcast.242, pred[]{:T(512)} %and_reduce_fusion.2), kind=kLoop, calls=%fused_computation.14.clone.1 | loop fusion | flops 131072 | bytes 786441 | tf_op jit(solution)/shard_map/select.79
  105.5 3.9 %fusion.114 = f32[9,256,256]{2,1,0:T(8,128)} fusion(f32[9,256,256]{2,1,0:T(8,128)} %get-tuple-element.612, bf16[9,16,16,256]{3,2,0,1:T(8,128)(2,1)S(1)} %copy-done.14, pred[]{:T(512)S(6)} %compare.180, pred[]{:T(512)S(6)} %and.121, bf16[16,16,256]{2,1,0:T(8,128)(2,1)} %copy-done.10), kind=kOutput, calls=%fused_computation.2.clone.1 | convolution fusion | flops 304349184 | bytes 6029314 | tf_op jit(solution)/shard_map/while/body/eval_jaxpr/krcd,rce->kde/dot_general | solution.py:49
  109.4 1.7 collective-permute-done
  121.3 2.0 %add_select_fusion.2 = f32[16,16,256]{2,1,0:T(8,128)S(1)} fusion(f32[9,16,16,256]{3,2,1,0:T(8,128)S(1)} %convolution_bitcast_fusion.2, f32[18,18,256]{2,1,0:T(8,128)S(1)} %scatter-add.71, s32[]{:T(128)} %bitcast.241, s32[]{:T(128)} %bitcast.242, pred[]{:T(512)} %and_reduce_fusion.2), kind=kLoop, calls=%fused_computation.14.clone.1 | loop fusion | flops 131072 | bytes 786441 | tf_op jit(solution)/shard_map/select.79
  129.2 3.9 %fusion.114 = f32[9,256,256]{2,1,0:T(8,128)} fusion(f32[9,256,256]{2,1,0:T(8,128)} %get-tuple-element.612, bf16[9,16,16,256]{3,2,0,1:T(8,128)(2,1)S(1)} %copy-done.14, pred[]{:T(512)S(6)} %compare.180, pred[]{:T(512)S(6)} %and.121, bf16[16,16,256]{2,1,0:T(8,128)(2,1)} %copy-done.10), kind=kOutput, calls=%fused_computation.2.clone.1 | convolution fusion | flops 304349184 | bytes 6029314 | tf_op jit(solution)/shard_map/while/body/eval_jaxpr/krcd,rce->kde/dot_general | solution.py:49
  133.0 1.7 collective-permute-done
  134.7 3.3 %fusion.57 = bf16[9,256,256]{2,1,0:T(8,128)(2,1)} fusion(f32[9,256,256]{2,1,0:T(8,128)} %get-tuple-element.472, bf16[1,1,9,256,256]{4,3,2,1,0:T(8,128)(2,1)} %param.29), kind=kLoop, calls=%fused_computation.74 | loop fusion | flops 2359296 | bytes 4718592 | tf_op jit(solution)/shard_map/convert_element_type | solution.py:93
  141.1 1.7 copy.19
  142.8 32.4 %all-reduce.4.cloned.1.call-done = bf16[9,256,256]{2,1,0:T(8,128)(2,1)} async-done(((bf16[9,256,256]{2,1,0:T(8,128)(2,1)}), bf16[9,256,256]{2,1,0:T(8,128)(2,1)}) %all-reduce.4.cloned.1.call-update) | async-done | bytes 1179664 | tf_op jit(solution)/shard_map/psum | solution.py:99
  175.2 3.9 %bitcast_add_fusion = (f32[9,256,256]{2,1,0:T(8,128)S(1)}, f32[1,9,256,256]{3,2,1,0:T(8,128)}) fusion(f32[9,4,64,256]{3,2,1,0:T(8,128)} %copy.19, bf16[9,256,256]{2,1,0:T(8,128)(2,1)} %all-reduce.4.cloned.1.call-done, f32[1,9,256,256]{3,2,1,0:T(8,128)S(1)} %copy-done.4), kind=kLoop, calls=%fused_computation.75 | loop fusion | flops 4128768 | bytes 10616832 | tf_op jit(solution)/shard_map/add | solution.py:101
  (302 shorter events, 77.2 us)
Async XLA Ops:
  7.2 168.0 %all-reduce.4.cloned.1.call-start = ((), (), s32[]{:S(2)}) async-start(), calls=%async_computation | async-start | bytes 2359296 | tf_op jit(solution)/shard_map/psum | solution.py:99
  7.2 3.4 %collective-permute-start.1 = (f32[1,9,64,256]{3,2,1,0:T(8,128)}, f32[1,9,64,256]{3,2,1,0:T(8,128)}, u32[]{:S(2)}, u32[]{:S(2)}) collective-permute-start(f32[1,9,64,256]{3,2,1,0:T(8,128)} %param.31), channel_id=1, source_target_pairs={{0,1},{1,0},{2,3},{3,2},{4,5},{5,4},{6,7},{7,6},{8,9},{9,8},{10,11... | collective-permute-start | bytes 1769480 | tf_op jit(solution)/shard_map/ppermute | solution.py:20
  13.2 124.9 %collective-permute-start.2 = (f32[2,9,64,256]{3,2,1,0:T(8,128)}, f32[2,9,64,256]{3,2,1,0:T(8,128)}, u32[]{:S(2)}, u32[]{:S(2)}) collective-permute-start(f32[2,9,64,256]{3,2,1,0:T(8,128)} %pad_maximum_fusion), channel_id=1, source_target_pairs={{0,2},{1,3},{2,0},{3,1},{4,6},{5,7},{6,4},{7,5},{8,10},{9,11},{10,... | collective-permute-start | bytes 3538952 | tf_op jit(solution)/shard_map/ppermute | solution.py:20
  15.8 4.7 %copy-start = (bf16[9,256,256]{2,1,0:T(8,128)(2,1)}, bf16[9,256,256]{2,1,0:T(8,128)(2,1)S(1)}, u32[]{:S(2)}) copy-start(bf16[9,256,256]{2,1,0:T(8,128)(2,1)S(1)} %get-tuple-element.634) | copy-start | bytes 3538948 | tf_op jit(solution)/shard_map/while
  32.6 7.5 %collective-permute-start = (bf16[16,16,256]{2,1,0:T(8,128)(2,1)S(1)}, bf16[16,16,256]{2,1,0:T(8,128)(2,1)S(1)}, u32[]{:S(2)}, u32[]{:S(2)}) collective-permute-start(bf16[16,16,256]{2,1,0:T(8,128)(2,1)S(1)} %fusion.113), channel_id=1, source_target_pairs={{4,0},{8,4},{12,8},{5,1},{9,5},{13,9},{6,2},{10,6},{14,10},{7,3},{... | collective-permute-start | bytes 393224 | tf_op jit(solution)/shard_map/while/body/eval_jaxpr/ppermute | solution.py:30
  33.9 6.2 %copy-start.1 = (bf16[9,256,256]{2,1,0:T(8,128)(2,1)S(1)}, bf16[9,256,256]{2,1,0:T(8,128)(2,1)}, u32[]{:S(2)}) copy-start(bf16[9,256,256]{2,1,0:T(8,128)(2,1)} %copy-done) | copy-start | bytes 3538948 | tf_op jit(solution)/shard_map/while
  33.9 6.2 %copy-start.3 = (bf16[2,16,16,256]{3,2,0,1:T(8,128)(2,1)S(1)}, bf16[2,16,16,256]{3,2,0,1:T(8,128)(2,1)}, u32[]{:S(2)}) copy-start(bf16[2,16,16,256]{3,2,0,1:T(8,128)(2,1)} %copy-done.2) | copy-start | bytes 786436 | tf_op jit(solution)/shard_map/while
  40.1 4.7 %copy-start = (bf16[9,256,256]{2,1,0:T(8,128)(2,1)}, bf16[9,256,256]{2,1,0:T(8,128)(2,1)S(1)}, u32[]{:S(2)}) copy-start(bf16[9,256,256]{2,1,0:T(8,128)(2,1)S(1)} %get-tuple-element.634) | copy-start | bytes 3538948 | tf_op jit(solution)/shard_map/while
  56.8 6.9 %collective-permute-start = (bf16[16,16,256]{2,1,0:T(8,128)(2,1)S(1)}, bf16[16,16,256]{2,1,0:T(8,128)(2,1)S(1)}, u32[]{:S(2)}, u32[]{:S(2)}) collective-permute-start(bf16[16,16,256]{2,1,0:T(8,128)(2,1)S(1)} %fusion.113), channel_id=1, source_target_pairs={{4,0},{8,4},{12,8},{5,1},{9,5},{13,9},{6,2},{10,6},{14,10},{7,3},{... | collective-permute-start | bytes 393224 | tf_op jit(solution)/shard_map/while/body/eval_jaxpr/ppermute | solution.py:30
  58.2 5.5 %copy-start.1 = (bf16[9,256,256]{2,1,0:T(8,128)(2,1)S(1)}, bf16[9,256,256]{2,1,0:T(8,128)(2,1)}, u32[]{:S(2)}) copy-start(bf16[9,256,256]{2,1,0:T(8,128)(2,1)} %copy-done) | copy-start | bytes 3538948 | tf_op jit(solution)/shard_map/while
  58.2 5.5 %copy-start.3 = (bf16[2,16,16,256]{3,2,0,1:T(8,128)(2,1)S(1)}, bf16[2,16,16,256]{3,2,0,1:T(8,128)(2,1)}, u32[]{:S(2)}) copy-start(bf16[2,16,16,256]{3,2,0,1:T(8,128)(2,1)} %copy-done.2) | copy-start | bytes 786436 | tf_op jit(solution)/shard_map/while
  63.7 4.7 %copy-start = (bf16[9,256,256]{2,1,0:T(8,128)(2,1)}, bf16[9,256,256]{2,1,0:T(8,128)(2,1)S(1)}, u32[]{:S(2)}) copy-start(bf16[9,256,256]{2,1,0:T(8,128)(2,1)S(1)} %get-tuple-element.634) | copy-start | bytes 3538948 | tf_op jit(solution)/shard_map/while
  80.5 6.9 %collective-permute-start = (bf16[16,16,256]{2,1,0:T(8,128)(2,1)S(1)}, bf16[16,16,256]{2,1,0:T(8,128)(2,1)S(1)}, u32[]{:S(2)}, u32[]{:S(2)}) collective-permute-start(bf16[16,16,256]{2,1,0:T(8,128)(2,1)S(1)} %fusion.113), channel_id=1, source_target_pairs={{4,0},{8,4},{12,8},{5,1},{9,5},{13,9},{6,2},{10,6},{14,10},{7,3},{... | collective-permute-start | bytes 393224 | tf_op jit(solution)/shard_map/while/body/eval_jaxpr/ppermute | solution.py:30
  81.8 5.5 %copy-start.1 = (bf16[9,256,256]{2,1,0:T(8,128)(2,1)S(1)}, bf16[9,256,256]{2,1,0:T(8,128)(2,1)}, u32[]{:S(2)}) copy-start(bf16[9,256,256]{2,1,0:T(8,128)(2,1)} %copy-done) | copy-start | bytes 3538948 | tf_op jit(solution)/shard_map/while
  81.8 5.5 %copy-start.3 = (bf16[2,16,16,256]{3,2,0,1:T(8,128)(2,1)S(1)}, bf16[2,16,16,256]{3,2,0,1:T(8,128)(2,1)}, u32[]{:S(2)}) copy-start(bf16[2,16,16,256]{3,2,0,1:T(8,128)(2,1)} %copy-done.2) | copy-start | bytes 786436 | tf_op jit(solution)/shard_map/while
  87.4 4.7 %copy-start = (bf16[9,256,256]{2,1,0:T(8,128)(2,1)}, bf16[9,256,256]{2,1,0:T(8,128)(2,1)S(1)}, u32[]{:S(2)}) copy-start(bf16[9,256,256]{2,1,0:T(8,128)(2,1)S(1)} %get-tuple-element.634) | copy-start | bytes 3538948 | tf_op jit(solution)/shard_map/while
  104.2 6.9 %collective-permute-start = (bf16[16,16,256]{2,1,0:T(8,128)(2,1)S(1)}, bf16[16,16,256]{2,1,0:T(8,128)(2,1)S(1)}, u32[]{:S(2)}, u32[]{:S(2)}) collective-permute-start(bf16[16,16,256]{2,1,0:T(8,128)(2,1)S(1)} %fusion.113), channel_id=1, source_target_pairs={{4,0},{8,4},{12,8},{5,1},{9,5},{13,9},{6,2},{10,6},{14,10},{7,3},{... | collective-permute-start | bytes 393224 | tf_op jit(solution)/shard_map/while/body/eval_jaxpr/ppermute | solution.py:30
  105.5 5.5 %copy-start.1 = (bf16[9,256,256]{2,1,0:T(8,128)(2,1)S(1)}, bf16[9,256,256]{2,1,0:T(8,128)(2,1)}, u32[]{:S(2)}) copy-start(bf16[9,256,256]{2,1,0:T(8,128)(2,1)} %copy-done) | copy-start | bytes 3538948 | tf_op jit(solution)/shard_map/while
  105.5 5.5 %copy-start.3 = (bf16[2,16,16,256]{3,2,0,1:T(8,128)(2,1)S(1)}, bf16[2,16,16,256]{3,2,0,1:T(8,128)(2,1)}, u32[]{:S(2)}) copy-start(bf16[2,16,16,256]{3,2,0,1:T(8,128)(2,1)} %copy-done.2) | copy-start | bytes 786436 | tf_op jit(solution)/shard_map/while
  111.0 4.7 %copy-start = (bf16[9,256,256]{2,1,0:T(8,128)(2,1)}, bf16[9,256,256]{2,1,0:T(8,128)(2,1)S(1)}, u32[]{:S(2)}) copy-start(bf16[9,256,256]{2,1,0:T(8,128)(2,1)S(1)} %get-tuple-element.634) | copy-start | bytes 3538948 | tf_op jit(solution)/shard_map/while
  127.8 6.9 %collective-permute-start = (bf16[16,16,256]{2,1,0:T(8,128)(2,1)S(1)}, bf16[16,16,256]{2,1,0:T(8,128)(2,1)S(1)}, u32[]{:S(2)}, u32[]{:S(2)}) collective-permute-start(bf16[16,16,256]{2,1,0:T(8,128)(2,1)S(1)} %fusion.113), channel_id=1, source_target_pairs={{4,0},{8,4},{12,8},{5,1},{9,5},{13,9},{6,2},{10,6},{14,10},{7,3},{... | collective-permute-start | bytes 393224 | tf_op jit(solution)/shard_map/while/body/eval_jaxpr/ppermute | solution.py:30
  129.1 5.5 %copy-start.1 = (bf16[9,256,256]{2,1,0:T(8,128)(2,1)S(1)}, bf16[9,256,256]{2,1,0:T(8,128)(2,1)}, u32[]{:S(2)}) copy-start(bf16[9,256,256]{2,1,0:T(8,128)(2,1)} %copy-done) | copy-start | bytes 3538948 | tf_op jit(solution)/shard_map/while
  129.2 5.5 %copy-start.3 = (bf16[2,16,16,256]{3,2,0,1:T(8,128)(2,1)S(1)}, bf16[2,16,16,256]{3,2,0,1:T(8,128)(2,1)}, u32[]{:S(2)}) copy-start(bf16[2,16,16,256]{3,2,0,1:T(8,128)(2,1)} %copy-done.2) | copy-start | bytes 786436 | tf_op jit(solution)/shard_map/while
  141.1 34.1 %copy-start.4 = (f32[1,9,256,256]{3,2,1,0:T(8,128)S(1)}, f32[1,9,256,256]{3,2,1,0:T(8,128)}, u32[]{:S(2)}) copy-start(f32[1,9,256,256]{3,2,1,0:T(8,128)} %param.30) | copy-start | bytes 7077892
  (37 other events, 75.8 us)
Sparse Core Ops, SparseCore 0:
  138.1 37.0 all-reduce.3
